TPU v7x, 256 devices: a whole 4x4x8 slice. The times are simulated.
256 devices in a mesh: aux: 16 (over x, y), occ: 16 (over z, core).
Axes of the slice: x: 4, y: 4, z: 8, core: 2. Of those that a mesh axis runs over, the one named last changes fastest.
Arguments:
- integrals: bfloat16 [32, 384, 128, 128], P('aux', 'occ'), may hold values from -1.5 to 1.5
- coefficients: bfloat16 [4096, 384], P('occ'), may hold values from -0.21875 to 0.21875
- pair_rows: int32 [16, 384], P('aux', 'occ'), may hold values from 0 to 1
- pair_cols: int32 [16, 384], P('aux', 'occ'), may hold values from 0 to 31
- pair_count: int32 [16, 16], P('aux', 'occ'), may hold values from 1 to 24, as said below
- row_blocks: int32 [32], replicated, may hold values from 0 to 31, each once
Outputs:
- exchange_matrix: float32 [4096, 4096], P('aux', 'occ')
Inputs may be any that keep to these rules, and one draw needn't show every extreme that they name: `pair_count`: at most 24 live slots for each auxiliary block and row owner, and some auxiliary block and owner has exactly 24.
All inputs are finite; a program needn't handle non-finite values.
Results may differ from a plain program's by a relative error of at most 0.0022.
Values may be sent and summed in bfloat16 or wider, within the bound.
A program may use at most 64 MiB of HBM per device.

v0:
```python
import jax
import jax.numpy as jnp
from jax import lax
from jax.sharding import PartitionSpec as P


def contract_rows(first, second):
    return jnp.einsum("pni,pmi->nm", first, second, preferred_element_type=jnp.float32)


def local(integrals, coefficients, pair_rows, pair_cols, pair_count, row_blocks):
    aux_count, slots, block_size, _ = integrals.shape
    block_total = row_blocks.shape[0]
    occ_size = lax.axis_size("occ")
    own_blocks = block_total // occ_size
    strip_width = own_blocks * block_size
    full_coeff = lax.all_gather(coefficients, "occ", axis=0, tiled=True)
    orbitals = full_coeff.shape[1]
    coeff_blocks = full_coeff.reshape(block_total, block_size, orbitals)
    basis_block = row_blocks[pair_cols[0]]
    gathered = jnp.take(coeff_blocks, basis_block, axis=0)
    live = jnp.arange(slots, dtype=jnp.int32) < pair_count[0, 0]
    placing = (pair_rows[0][None, :] == jnp.arange(own_blocks, dtype=jnp.int32)[:, None]) & live[
        None, :
    ]
    weights = jnp.where(placing[:, :, None, None], gathered[None], jnp.zeros((), gathered.dtype))
    summed_half = jnp.einsum(
        "psmn,rsni->prmi", integrals, weights, preferred_element_type=jnp.float32
    )
    half = summed_half.reshape(aux_count, strip_width, orbitals).astype(jnp.bfloat16)
    strip = contract_rows(lax.all_gather(half, "occ", axis=1, tiled=True), half)
    return lax.psum_scatter(strip, "aux", scatter_dimension=0, tiled=True)


def solution(mesh):
    return jax.shard_map(
        local,
        mesh=mesh,
        in_specs=(
            P("aux", "occ", None, None),
            P("occ", None),
            P("aux", "occ"),
            P("aux", "occ"),
            P("aux", "occ"),
            P(),
        ),
        out_specs=P("aux", "occ"),
        check_vma=False,
    )
```

profile of v0, /device:TPU:2, one launch (start us, length us, event | category | flops | bytes accessed | tf_op | source)
XLA Modules:
  0.0 201.0 jit_solution(10329253605268713100)
XLA Ops:
  6.5 0.0 copy-start
  6.5 0.0 all-gather.3.cloned.1.call-start
  6.5 0.7 all-gather.3.cloned.1.call-update
  7.3 0.0 all-gather.5.cloned.1.call-start
  8.0 0.7 fusion.22
  8.6 1.4 gather_fusion
  10.0 0.7 compare_and_fusion.1
  10.7 42.5 %all-gather.3.cloned.1.call-done = bf16[4096,384]{1,0:T(8,128)(2,1)} async-done(((bf16[256,384]{1,0:T(8,128)(2,1)}), bf16[4096,384]{1,0:T(8,128)(2,1)}) %all-gather.3.cloned.1.call-update) | async-done | bytes 3145744 | tf_op jit(solution)/shard_map/all_gather | solution.py:17
  53.2 4.4 %gather_fusion.1 = bf16[24,128,384]{2,1,0:T(8,128)(2,1)} fusion(bf16[32,128,384]{2,1,0:T(8,128)(2,1)} %bitcast.48, s32[1024]{0:T(1024)S(1)} %pad_clamp_fusion), kind=kCustom, calls=%fused_computation.1 | custom fusion | bytes 4718688 | tf_op jit(solution)/shard_map/jit(_take)/gather | solution.py:21
  57.5 2.0 broadcast_select_fusion
  59.5 0.0 copy-done
  59.5 1.5 fusion.17
  61.0 0.8 copy.7
  61.8 0.0 all-gather.5.cloned.1.call-update
  61.8 0.0 reduce-scatter.2.cloned.1.call-start
  61.9 44.8 %all-gather.5.cloned.1.call-done = bf16[2,4096,384]{2,1,0:T(8,128)(2,1)} async-done(((bf16[2,256,384]{2,1,0:T(8,128)(2,1)}), bf16[2,4096,384]{2,1,0:T(8,128)(2,1)}) %all-gather.5.cloned.1.call-update) | async-done | bytes 6291472 | tf_op jit(solution)/shard_map/all_gather | solution.py:31
  106.7 6.7 %convolution_bitcast_fusion = f32[4096,256]{1,0:T(8,128)} fusion(bf16[2,4096,384]{2,1,0:T(8,128)(2,1)} %all-gather.5.cloned.1.call-done, bf16[2,256,384]{2,1,0:T(8,128)(2,1)} %bitcast.47), kind=kOutput, calls=%fused_computation.2 | convolution fusion | flops 1610612736 | bytes 10878976 | tf_op jit(solution)/shard_map/pni,pmi->nm/dot_general | solution.py:8
  113.3 0.0 reduce-scatter.2.cloned.1.call-update
  113.3 81.1 %reduce-scatter.2.cloned.1.call-done = f32[256,256]{1,0:T(8,128)} async-done(((f32[4096,256]{1,0:T(8,128)}), f32[256,256]{1,0:T(8,128)}) %reduce-scatter.2.cloned.1.call-update) | async-done | bytes 262160 | tf_op jit(solution)/shard_map/reduce_scatter | solution.py:32
  (5 shorter events, 0.0 us)
Async XLA Ops:
  6.5 53.0 %copy-start = (bf16[2,24,128,128]{3,2,1,0:T(8,128)(2,1)S(1)}, bf16[2,24,128,128]{3,2,1,0:T(8,128)(2,1)}, u32[]{:S(2)}) copy-start(bf16[2,24,128,128]{3,2,1,0:T(8,128)(2,1)} %param.6) | copy-start | bytes 4718596
  6.5 46.6 %all-gather.3.cloned.1.call-start = ((), (), s32[]{:S(2)}) async-start(), calls=%async_computation.1 | async-start | bytes 3342336 | tf_op jit(solution)/shard_map/all_gather | solution.py:17
  7.3 99.4 %all-gather.5.cloned.1.call-start = ((), (), s32[]{:S(2)}) async-start(), calls=%async_computation.2 | async-start | bytes 6684672 | tf_op jit(solution)/shard_map/all_gather | solution.py:31
  61.8 132.6 %reduce-scatter.2.cloned.1.call-start = ((), (), s32[]{:S(2)}) async-start(), calls=%async_computation.3 | async-start | bytes 4456448 | tf_op jit(solution)/shard_map/reduce_scatter | solution.py:32
Sparse Core Ops, SparseCore 0:
  9.2 43.9 all-gather.2
  62.0 44.6 all-gather.4
  113.5 80.9 reduce-scatter.1
where the time goes:
time: 201 us
  waiting for transfers between devices  169 us (84%)
  between operations  13.8 us (7%)
  matrix products  8.13 us (4%)
  local copies, waits for them, and re-layouts  6.52 us (3%)
  other arithmetic  3.35 us (2%)
    reduce_scatter x1, waiting for transfers between devices, local(): return lax.psum_scatter(strip, 'aux', scatter_dimension=0, tiled=True)  81.1 us
    all_gather x1, waiting for transfers between devices, local(): strip = contract_rows(lax.all_gather(half, 'occ', axis=1, tiled=True), half)  44.8 us
    all_gather x1, waiting for transfers between devices, local(): full_coeff = lax.all_gather(coefficients, 'occ', axis=0, tiled=True)  42.5 us
    dot_general x1, matrix products, contract_rows(): jnp.einsum('pni,pmi->nm', first, second, preferred_element_type=jnp.float32)  6.66 us
    gather x1, local copies, waits for them, and re-layouts, local(): gathered = jnp.take(coeff_blocks, basis_block, axis=0)  4.35 us
  transfers between devices with their start and end apart: 3, of which 3 were waited for; matrix products, arithmetic and copies ran while one was open for 1% of the time, Pallas kernels for 0%

commit v1 on v0

--- a/solution.py
+++ b/solution.py
@@ -2,6 +2,12 @@
 import jax.numpy as jnp
 from jax import lax
 from jax.sharding import PartitionSpec as P
+
+
+def gather_from_all(x, axis, dim):
+    count = lax.axis_size(axis)
+    repeats = [count if d == dim else 1 for d in range(x.ndim)]
+    return lax.all_to_all(jnp.tile(x, repeats), axis, split_axis=dim, concat_axis=dim, tiled=True)
 
 
 def contract_rows(first, second):
@@ -28,7 +34,7 @@
         "psmn,rsni->prmi", integrals, weights, preferred_element_type=jnp.float32
     )
     half = summed_half.reshape(aux_count, strip_width, orbitals).astype(jnp.bfloat16)
-    strip = contract_rows(lax.all_gather(half, "occ", axis=1, tiled=True), half)
+    strip = contract_rows(gather_from_all(half, "occ", 1), half)
     return lax.psum_scatter(strip, "aux", scatter_dimension=0, tiled=True)
 
 

time: 201 us -> 302 us (1.50)
  blocking collectives: 0 us -> 144 us
  waiting for transfers between devices: 169 us -> 124 us
  local copies, waits for them, and re-layouts: 6.52 us -> 11.2 us
    all_to_all x0 -> x1, blocking collectives: none -> 144 us  [gather_from_all(): lax.all_to_all(jnp.tile(x, repeats), axis, split_axis=dim, concat_axis=di...]
    all_gather x1 -> x0, waiting for transfers between devices: 44.8 us -> none  [local(): strip = contract_rows(lax.all_gather(half, 'occ', axis=1, tiled=True), half)]
    another operation x0 -> x1, local copies, waits for them, and re-layouts: none -> 5.06 us  [gather_from_all(): jnp.tile(x, repeats)]
  transfers between devices with their start and end apart: 3 -> 2, of which waited for: 3 -> 2; matrix products, arithmetic and copies ran while one was open for 1% -> 1% of each run, Pallas kernels for 0% -> 0%
where the time goes in v1:
time: 302 us
  blocking collectives  144 us (48%)
  waiting for transfers between devices  124 us (41%)
  between operations  14.1 us (5%)
  local copies, waits for them, and re-layouts  11.2 us (4%)
  matrix products  5.26 us (2%)
  other arithmetic  3.35 us (1%)
    all_to_all x1, blocking collectives, gather_from_all(): lax.all_to_all(jnp.tile(x, repeats), axis, split_axis=dim, concat_axis=di...  144 us
    reduce_scatter x1, waiting for transfers between devices, local(): return lax.psum_scatter(strip, 'aux', scatter_dimension=0, tiled=True)  80.9 us
    all_gather x1, waiting for transfers between devices, local(): full_coeff = lax.all_gather(coefficients, 'occ', axis=0, tiled=True)  42.5 us
  transfers between devices with their start and end apart: 2, of which 2 were waited for; matrix products, arithmetic and copies ran while one was open for 1% of the time, Pallas kernels for 0%

profile of v1, /device:TPU:2, one launch (start us, length us, event | category | flops | bytes accessed | tf_op | source)
XLA Modules:
  0.0 301.9 jit_solution(18211739926151828311)
XLA Ops:
  6.5 0.0 copy-start
  6.5 0.0 all-gather.2.cloned.1.call-start
  6.5 0.7 all-gather.2.cloned.1.call-update
  7.3 0.0 reduce-scatter.2.cloned.1.call-start
  8.0 0.7 fusion.27
  8.6 1.4 gather_fusion
  10.0 0.7 compare_and_fusion.1
  10.7 42.5 %all-gather.2.cloned.1.call-done = bf16[4096,384]{1,0:T(8,128)(2,1)} async-done(((bf16[256,384]{1,0:T(8,128)(2,1)}), bf16[4096,384]{1,0:T(8,128)(2,1)}) %all-gather.2.cloned.1.call-update) | async-done | bytes 3145744 | tf_op jit(solution)/shard_map/all_gather | solution.py:23
  53.2 4.3 %gather_fusion.1 = bf16[24,128,384]{2,1,0:T(8,128)(2,1)} fusion(bf16[32,128,384]{2,1,0:T(8,128)(2,1)} %bitcast.47, s32[1024]{0:T(1024)S(1)} %pad_clamp_fusion), kind=kCustom, calls=%fused_computation.1 | custom fusion | bytes 4718688 | tf_op jit(solution)/shard_map/jit(_take)/gather | solution.py:27
  57.5 2.0 broadcast_select_fusion
  59.5 0.0 copy-done
  59.5 1.5 fusion.22
  61.0 0.4 copy.9
  61.4 5.1 %tile.4 = bf16[2,16,256,384]{3,0,2,1:T(2,128)(2,1)S(1)} broadcast(bf16[2,256,384]{2,0,1:T(2,128)(2,1)S(1)} %copy.9), dimensions={0,2,3} | broadcast | bytes 6684672 | tf_op jit(solution)/shard_map/tile | solution.py:10
  66.5 143.9 %all_to_all.5 = bf16[2,4096,384]{2,0,1:T(2,128)(2,1)S(1)} all-to-all(bf16[2,4096,384]{2,0,1:T(2,128)(2,1)S(1)} %bitcast.46), channel_id=1, replica_groups=mesh['aux'=16,'occ'=16] {'occ'}, dimensions={1} | all-to-all | bytes 12582912 | tf_op jit(solution)/shard_map/all_to_all | solution.py:10
  210.4 3.8 %fusion.2 = f32[4096,256]{1,0:T(8,128)} fusion(bf16[2,256,384]{2,1,0:T(8,128)(2,1)S(1)} %bitcast.49, bf16[2,4096,384]{2,0,1:T(2,128)(2,1)S(1)} %all_to_all.5), kind=kOutput, calls=%fused_computation.4 | convolution fusion | flops 1610612736 | bytes 10878976 | tf_op jit(solution)/shard_map/pni,pmi->nm/dot_general | solution.py:14
  214.2 0.0 reduce-scatter.2.cloned.1.call-update
  214.2 80.9 %reduce-scatter.2.cloned.1.call-done = f32[256,256]{1,0:T(8,128)} async-done(((f32[4096,256]{1,0:T(8,128)}), f32[256,256]{1,0:T(8,128)}) %reduce-scatter.2.cloned.1.call-update) | async-done | bytes 262160 | tf_op jit(solution)/shard_map/reduce_scatter | solution.py:38
  (6 shorter events, 0.1 us)
Async XLA Ops:
  6.5 53.0 %copy-start = (bf16[2,24,128,128]{3,2,1,0:T(8,128)(2,1)S(1)}, bf16[2,24,128,128]{3,2,1,0:T(8,128)(2,1)}, u32[]{:S(2)}) copy-start(bf16[2,24,128,128]{3,2,1,0:T(8,128)(2,1)} %param.6) | copy-start | bytes 4718596
  6.5 46.6 %all-gather.2.cloned.1.call-start = ((), (), s32[]{:S(2)}) async-start(), calls=%async_computation.2 | async-start | bytes 3342336 | tf_op jit(solution)/shard_map/all_gather | solution.py:23
  7.3 287.8 %reduce-scatter.2.cloned.1.call-start = ((), (), s32[]{:S(2)}) async-start(), calls=%async_computation.3 | async-start | bytes 4456448 | tf_op jit(solution)/shard_map/reduce_scatter | solution.py:38
Sparse Core Ops, SparseCore 0:
  9.2 43.9 all-gather.1
  214.3 80.6 reduce-scatter.1
